TPU v7x, 256 devices: a whole 4x4x8 slice. The times are simulated.
256 devices in a mesh: gx: 32 (over x, z), gy: 8 (over y, core).
Axes of the slice: x: 4, y: 4, z: 8, core: 2. Of those that a mesh axis runs over, the one named last changes fastest.
Arguments:
- flow_state: float32 [4, 4096, 1024], P(None, 'gx', 'gy'), may hold values from -6 to 6
- sound_speed_sq: float32 [4096, 1024], P('gx', 'gy'), may hold values from 0.25 to 1
- snapshots: bfloat16 [62, 4096, 1024], P(None, 'gx', 'gy'), may hold values from -96 to 96
Outputs:
- new_state: float32 [4, 4096, 1024], P(None, 'gx', 'gy')
- pod_basis: float32 [64, 4096, 1024], P(None, 'gx', 'gy')
All inputs are finite; a program needn't handle non-finite values.
Results may differ from a plain program's by a relative error of at most 0.00063.
Values sent between devices are 32-bit elements; how exact they have to be, the bound alone decides.
A program may use at most 64 MiB of HBM per device.

v0:
```python
import jax
import jax.numpy as jnp
from jax import lax
from jax.sharding import PartitionSpec as P

STEPS = 2
courant = 0.8
stream_speed = 0.3
span_speed = 0.1


def padded_2(block, sides, width):
    for axis, dim in sides:
        count = lax.axis_size(axis)
        forward = [(i, i + 1) for i in range(count - 1)]
        forward.append((count - 1, 0))
        backward = [(target, source) for source, target in forward]
        low = lax.ppermute(
            lax.slice_in_dim(block, block.shape[dim] - width, None, axis=dim), axis, forward
        )
        high = lax.ppermute(lax.slice_in_dim(block, 0, width, axis=dim), axis, backward)
        block = jnp.concatenate([low, block, high], axis=dim)
    return block


def derivative_x(padded):
    interior = padded[:, :, 2:-2]
    extent = interior.shape[1] - 4
    ahead_one = interior[:, 3 : 3 + extent]
    behind_one = interior[:, 1 : 1 + extent]
    ahead_two = interior[:, 4 : 4 + extent]
    behind_two = interior[:, 0:extent]
    return (8.0 * (ahead_one - behind_one) - (ahead_two - behind_two)) / 12.0


def derivative_y(padded):
    interior = padded[:, 2:-2, :]
    extent = interior.shape[2] - 4
    ahead_one = interior[:, :, 3 : 3 + extent]
    behind_one = interior[:, :, 1 : 1 + extent]
    ahead_two = interior[:, :, 4 : 4 + extent]
    behind_two = interior[:, :, 0:extent]
    return (8.0 * (ahead_one - behind_one) - (ahead_two - behind_two)) / 12.0


def tendency(padded, sound_sq):
    slope_x = derivative_x(padded)
    slope_y = derivative_y(padded)
    advect = stream_speed * slope_x + span_speed * slope_y
    diverge = slope_x[1] + slope_y[2]
    rate_rho = -courant * (advect[0] + diverge)
    rate_mx = -courant * (advect[1] + slope_x[3])
    rate_my = -courant * (advect[2] + slope_y[3])
    rate_p = -courant * (advect[3] + sound_sq * diverge)
    return jnp.stack([rate_rho, rate_mx, rate_my, rate_p])


def extend(current):
    return padded_2(current, (("gx", 1), ("gy", 2)), 2)


def advance(current, sound_sq):
    first = current + tendency(extend(current), sound_sq)
    second = 0.75 * current + 0.25 * (first + tendency(extend(first), sound_sq))
    return 1.0 / 3.0 * current + 2.0 / 3.0 * (second + tendency(extend(second), sound_sq))


def body(flow_state, sound_speed_sq, snapshots):
    current = flow_state
    columns = [snapshots]
    for step_index in range(STEPS):
        current = advance(current, sound_speed_sq)
        columns.append(current[3].astype(jnp.bfloat16)[None])
    snap_block = jnp.concatenate(columns, axis=0)
    mode_count = snap_block.shape[0]
    flat_block = snap_block.reshape(mode_count, -1)
    cell_total = flat_block.shape[1] * lax.axis_size("gx") * lax.axis_size("gy")
    local_gram = (
        lax.dot_general(
            flat_block, flat_block, (((1,), (1,)), ((), ())), preferred_element_type=jnp.float32
        )
        / cell_total
    )
    gram = lax.psum(local_gram, ("gx", "gy"))
    lower_factor = jnp.linalg.cholesky(gram)
    identity_matrix = jnp.eye(mode_count, dtype=jnp.float32)
    inverse = jax.scipy.linalg.solve_triangular(lower_factor, identity_matrix, lower=True)
    pod_basis = jnp.dot(inverse, flat_block.astype(jnp.float32), precision=lax.Precision.HIGHEST)
    return (current, pod_basis.reshape(snap_block.shape))


def solution(mesh):
    placed = (P(None, "gx", "gy"), P("gx", "gy"), P(None, "gx", "gy"))
    return jax.shard_map(
        body,
        mesh=mesh,
        in_specs=placed,
        out_specs=(P(None, "gx", "gy"), P(None, "gx", "gy")),
        check_vma=False,
    )
```

profile of v0, /device:TPU:1, one launch (start us, length us, event | category | flops | bytes accessed | tf_op | source)
XLA Modules:
  0.0 197.1 jit_solution(15976753331273612163)
XLA Ops:
  0.6 0.8 fusion.139
  1.4 2.5 %collective-permute-start.1 = (f32[4,2,128]{2,1,0:T(2,128)S(1)}, f32[4,2,128]{2,1,0:T(2,128)S(1)}, u32[]{:S(2)}, u32[]{:S(2)}) collective-permute-start(f32[4,2,128]{2,1,0:T(2,128)S(1)} %get-tuple-element.73), channel_id=1, source_target_pairs={{0,8},{8,16},{16,24},{24,32},{32,40},{40,48},{48,56},{56,64},{64,7... | collective-permute-start | bytes 12296 | tf_op jit(solution)/shard_map/ppermute | solution.py:18
  3.9 6.2 %collective-permute-start = (f32[4,2,128]{2,1,0:T(2,128)S(1)}, f32[4,2,128]{2,1,0:T(2,128)S(1)}, u32[]{:S(2)}, u32[]{:S(2)}) collective-permute-start(f32[4,2,128]{2,1,0:T(2,128)S(1)} %get-tuple-element.74), channel_id=1, source_target_pairs={{8,0},{16,8},{24,16},{32,24},{40,32},{48,40},{56,48},{64,56},{72,6... | collective-permute-start | bytes 12296 | tf_op jit(solution)/shard_map/ppermute | solution.py:21
  10.1 0.9 collective-permute-done.1
  11.0 1.0 pad_maximum_fusion
  12.2 1.6 collective-permute-start.2
  13.7 1.2 collective-permute-start.3
  14.9 4.5 %collective-permute-done.2 = f32[4,132,2]{2,1,0:T(8,128)S(1)} collective-permute-done((f32[4,132,2]{2,1,0:T(8,128)S(1)}, f32[4,132,2]{2,1,0:T(8,128)S(1)}, u32[]{:S(2)}, u32[]{:S(2)}) %collective-permute-start.2) | collective-permute-done | bytes 4256 | tf_op jit(solution)/shard_map/ppermute | solution.py:21
  19.4 2.0 %broadcast_multiply_fusion.10 = (f32[4,128,128]{2,1,0:T(8,128)S(1)}, f32[4,128,128]{2,1,0:T(8,128)S(1)}, f32[4,130,128]{2,1,0:T(8,128)S(1)}) fusion(f32[4,2,128]{2,1,0:T(2,128)S(1)} %collective-permute-done, f32[4,128,128]{2,1,0:T(8,128)} %param.3, f32[4,2,128]{2,1,0:T(2,128)S(1)} %collective-permute-done.1, f32[4,132,2]{2,1,0:T(8,128)S(1)} %collective-permute-done.3, ...), kind=kLoop, calls=%fused_computation.177 | loop fusion | flops 1114111 | bytes 1065216 | tf_op jit(solution)/shard_map/div | solution.py:43
  21.8 5.2 %collective-permute-start.4 = (f32[4,2,128]{2,1,0:T(2,128)S(1)}, f32[4,2,128]{2,1,0:T(2,128)S(1)}, u32[]{:S(2)}, u32[]{:S(2)}) collective-permute-start(f32[4,2,128]{2,1,0:T(2,128)S(1)} %get-tuple-element.71), channel_id=1, source_target_pairs={{8,0},{16,8},{24,16},{32,24},{40,32},{48,40},{56,48},{64,56},{72,6... | collective-permute-start | bytes 12296 | tf_op jit(solution)/shard_map/ppermute | solution.py:21
  27.0 0.9 collective-permute-done.5
  28.1 3.9 %collective-permute-start.6 = (f32[4,132,2]{2,1,0:T(8,128)S(1)}, f32[4,132,2]{2,1,0:T(8,128)S(1)}, u32[]{:S(2)}, u32[]{:S(2)}) collective-permute-start(f32[4,132,2]{2,1,0:T(8,128)S(1)} %get-tuple-element.58), channel_id=1, source_target_pairs={{1,0},{2,1},{3,2},{4,3},{5,4},{6,5},{7,6},{0,7},{9,8},{10,9},{11,1... | collective-permute-start | bytes 12680 | tf_op jit(solution)/shard_map/ppermute | solution.py:21
  32.1 2.6 %collective-permute-done.6 = f32[4,132,2]{2,1,0:T(8,128)S(1)} collective-permute-done((f32[4,132,2]{2,1,0:T(8,128)S(1)}, f32[4,132,2]{2,1,0:T(8,128)S(1)}, u32[]{:S(2)}, u32[]{:S(2)}) %collective-permute-start.6) | collective-permute-done | bytes 4256 | tf_op jit(solution)/shard_map/ppermute | solution.py:21
  34.7 0.8 collective-permute-done.7
  35.5 0.6 broadcast_multiply_fusion.8
  36.3 5.1 %collective-permute-start.8 = (f32[4,2,128]{2,1,0:T(2,128)S(1)}, f32[4,2,128]{2,1,0:T(2,128)S(1)}, u32[]{:S(2)}, u32[]{:S(2)}) collective-permute-start(f32[4,2,128]{2,1,0:T(2,128)S(1)} %get-tuple-element.69), channel_id=1, source_target_pairs={{8,0},{16,8},{24,16},{32,24},{40,32},{48,40},{56,48},{64,56},{72,6... | collective-permute-start | bytes 12296 | tf_op jit(solution)/shard_map/ppermute | solution.py:21
  41.5 0.9 collective-permute-done.9
  42.6 4.6 %collective-permute-start.10 = (f32[4,132,2]{2,1,0:T(8,128)S(1)}, f32[4,132,2]{2,1,0:T(8,128)S(1)}, u32[]{:S(2)}, u32[]{:S(2)}) collective-permute-start(f32[4,132,2]{2,1,0:T(8,128)S(1)} %get-tuple-element.56), channel_id=1, source_target_pairs={{1,0},{2,1},{3,2},{4,3},{5,4},{6,5},{7,6},{0,7},{9,8},{10,9},{11,1... | collective-permute-start | bytes 12680 | tf_op jit(solution)/shard_map/ppermute | solution.py:21
  47.3 2.9 %collective-permute-done.10 = f32[4,132,2]{2,1,0:T(8,128)S(1)} collective-permute-done((f32[4,132,2]{2,1,0:T(8,128)S(1)}, f32[4,132,2]{2,1,0:T(8,128)S(1)}, u32[]{:S(2)}, u32[]{:S(2)}) %collective-permute-start.10) | collective-permute-done | bytes 4256 | tf_op jit(solution)/shard_map/ppermute | solution.py:21
  50.1 0.5 collective-permute-done.11
  50.6 0.6 broadcast_multiply_fusion.6
  51.5 5.2 %collective-permute-start.12 = (f32[4,2,128]{2,1,0:T(2,128)S(1)}, f32[4,2,128]{2,1,0:T(2,128)S(1)}, u32[]{:S(2)}, u32[]{:S(2)}) collective-permute-start(f32[4,2,128]{2,1,0:T(2,128)S(1)} %get-tuple-element.67), channel_id=1, source_target_pairs={{8,0},{16,8},{24,16},{32,24},{40,32},{48,40},{56,48},{64,56},{72,6... | collective-permute-start | bytes 12296 | tf_op jit(solution)/shard_map/ppermute | solution.py:21
  56.8 0.9 collective-permute-done.13
  57.9 4.6 %collective-permute-start.14 = (f32[4,132,2]{2,1,0:T(8,128)S(1)}, f32[4,132,2]{2,1,0:T(8,128)S(1)}, u32[]{:S(2)}, u32[]{:S(2)}) collective-permute-start(f32[4,132,2]{2,1,0:T(8,128)S(1)} %get-tuple-element.54), channel_id=1, source_target_pairs={{1,0},{2,1},{3,2},{4,3},{5,4},{6,5},{7,6},{0,7},{9,8},{10,9},{11,1... | collective-permute-start | bytes 12680 | tf_op jit(solution)/shard_map/ppermute | solution.py:21
  62.6 2.9 %collective-permute-done.14 = f32[4,132,2]{2,1,0:T(8,128)S(1)} collective-permute-done((f32[4,132,2]{2,1,0:T(8,128)S(1)}, f32[4,132,2]{2,1,0:T(8,128)S(1)}, u32[]{:S(2)}, u32[]{:S(2)}) %collective-permute-start.14) | collective-permute-done | bytes 4256 | tf_op jit(solution)/shard_map/ppermute | solution.py:21
  65.5 0.5 collective-permute-done.15
  65.9 0.6 broadcast_multiply_fusion.4
  66.8 5.4 %collective-permute-start.16 = (f32[4,2,128]{2,1,0:T(2,128)S(1)}, f32[4,2,128]{2,1,0:T(2,128)S(1)}, u32[]{:S(2)}, u32[]{:S(2)}) collective-permute-start(f32[4,2,128]{2,1,0:T(2,128)S(1)} %get-tuple-element.65), channel_id=1, source_target_pairs={{8,0},{16,8},{24,16},{32,24},{40,32},{48,40},{56,48},{64,56},{72,6... | collective-permute-start | bytes 12296 | tf_op jit(solution)/shard_map/ppermute | solution.py:21
  72.2 1.3 copy.66
  73.8 1.4 copy.76
  75.4 4.0 %collective-permute-start.18 = (f32[4,132,2]{2,1,0:T(8,128)S(1)}, f32[4,132,2]{2,1,0:T(8,128)S(1)}, u32[]{:S(2)}, u32[]{:S(2)}) collective-permute-start(f32[4,132,2]{2,1,0:T(8,128)S(1)} %get-tuple-element.52), channel_id=1, source_target_pairs={{1,0},{2,1},{3,2},{4,3},{5,4},{6,5},{7,6},{0,7},{9,8},{10,9},{11,1... | collective-permute-start | bytes 12680 | tf_op jit(solution)/shard_map/ppermute | solution.py:21
  79.5 2.9 %collective-permute-done.18 = f32[4,132,2]{2,1,0:T(8,128)S(1)} collective-permute-done((f32[4,132,2]{2,1,0:T(8,128)S(1)}, f32[4,132,2]{2,1,0:T(8,128)S(1)}, u32[]{:S(2)}, u32[]{:S(2)}) %collective-permute-start.18) | collective-permute-done | bytes 4256 | tf_op jit(solution)/shard_map/ppermute | solution.py:21
  82.4 0.5 collective-permute-done.19
  82.9 0.6 broadcast_multiply_fusion.2
  83.7 4.8 %collective-permute-start.20 = (f32[4,2,128]{2,1,0:T(2,128)S(1)}, f32[4,2,128]{2,1,0:T(2,128)S(1)}, u32[]{:S(2)}, u32[]{:S(2)}) collective-permute-start(f32[4,2,128]{2,1,0:T(2,128)S(1)} %get-tuple-element.63), channel_id=1, source_target_pairs={{8,0},{16,8},{24,16},{32,24},{40,32},{48,40},{56,48},{64,56},{72,6... | collective-permute-start | bytes 12296 | tf_op jit(solution)/shard_map/ppermute | solution.py:21
  88.6 0.9 collective-permute-done.21
  89.7 4.9 %collective-permute-start.22 = (f32[4,132,2]{2,1,0:T(8,128)S(1)}, f32[4,132,2]{2,1,0:T(8,128)S(1)}, u32[]{:S(2)}, u32[]{:S(2)}) collective-permute-start(f32[4,132,2]{2,1,0:T(8,128)S(1)} %get-tuple-element.50), channel_id=1, source_target_pairs={{1,0},{2,1},{3,2},{4,3},{5,4},{6,5},{7,6},{0,7},{9,8},{10,9},{11,1... | collective-permute-start | bytes 12680 | tf_op jit(solution)/shard_map/ppermute | solution.py:21
  94.7 2.9 %collective-permute-done.22 = f32[4,132,2]{2,1,0:T(8,128)S(1)} collective-permute-done((f32[4,132,2]{2,1,0:T(8,128)S(1)}, f32[4,132,2]{2,1,0:T(8,128)S(1)}, u32[]{:S(2)}, u32[]{:S(2)}) %collective-permute-start.22) | collective-permute-done | bytes 4256 | tf_op jit(solution)/shard_map/ppermute | solution.py:21
  97.5 0.5 collective-permute-done.23
  98.0 0.6 broadcast_multiply_fusion
  98.9 0.7 fusion.12
  99.6 78.8 %psum.7 = f32[64,64]{0,1:T(8,128)S(1)} all-reduce(f32[64,64]{0,1:T(8,128)S(1)} %fusion.12), channel_id=1, replica_groups=mesh['gx'=32,'gy'=8] {'gx','gy'}, use_global_device_ids=true, to_apply=%region_0.0 | all-reduce | flops 4096 | bytes 32768 | tf_op jit(solution)/shard_map/psum | solution.py:84
  178.5 5.8 %cholesky.17 = f32[64,64]{1,0:T(8,128)S(1)} custom-call(f32[64,64]{1,0:T(8,128)S(1)} %fusion.114), custom_call_target="Cholesky" | custom-call | tf_op jit(solution)/shard_map/jit(cholesky)/cholesky | solution.py:85
  184.4 0.6 compare_reduce_fusion
  185.0 0.7 fusion.112
  185.7 4.9 %custom-call.7 = f32[1,64,64]{1,2,0:T(8,128)S(1)} custom-call(f32[1,64,64]{2,1,0:T(8,128)S(1)} %fusion.112), custom_call_target="InvertDiagBlocksLowerTriangular" | custom-call | tf_op jit(solution)/shard_map/jit(_solve_triangular)/triangular_solve | solution.py:87
  190.9 1.8 fusion
  192.7 4.4 %copy.72 = f32[64,128,128]{2,1,0:T(8,128)} copy(f32[64,128,128]{2,0,1:T(8,128)S(1)} %fusion) | data formatting | bytes 8388608
  (85 shorter events, 4.0 us)
Async XLA Ops:
  0.6 20.8 %copy-start = (f32[4,128,128]{2,1,0:T(8,128)S(1)}, f32[4,128,128]{2,1,0:T(8,128)}, u32[]{:S(2)}) copy-start(f32[4,128,128]{2,1,0:T(8,128)} %param.3) | copy-start | bytes 786436
  1.4 9.6 %collective-permute-start.1 = (f32[4,2,128]{2,1,0:T(2,128)S(1)}, f32[4,2,128]{2,1,0:T(2,128)S(1)}, u32[]{:S(2)}, u32[]{:S(2)}) collective-permute-start(f32[4,2,128]{2,1,0:T(2,128)S(1)} %get-tuple-element.73), channel_id=1, source_target_pairs={{0,8},{8,16},{16,24},{24,32},{32,40},{40,48},{48,56},{56,64},{64,7... | collective-permute-start | bytes 12296 | tf_op jit(solution)/shard_map/ppermute | solution.py:18
  3.9 7.1 %collective-permute-start = (f32[4,2,128]{2,1,0:T(2,128)S(1)}, f32[4,2,128]{2,1,0:T(2,128)S(1)}, u32[]{:S(2)}, u32[]{:S(2)}) collective-permute-start(f32[4,2,128]{2,1,0:T(2,128)S(1)} %get-tuple-element.74), channel_id=1, source_target_pairs={{8,0},{16,8},{24,16},{32,24},{40,32},{48,40},{56,48},{64,56},{72,6... | collective-permute-start | bytes 12296 | tf_op jit(solution)/shard_map/ppermute | solution.py:21
  12.2 7.3 %collective-permute-start.2 = (f32[4,132,2]{2,1,0:T(8,128)S(1)}, f32[4,132,2]{2,1,0:T(8,128)S(1)}, u32[]{:S(2)}, u32[]{:S(2)}) collective-permute-start(f32[4,132,2]{2,1,0:T(8,128)S(1)} %get-tuple-element.60), channel_id=1, source_target_pairs={{1,0},{2,1},{3,2},{4,3},{5,4},{6,5},{7,6},{0,7},{9,8},{10,9},{11,1... | collective-permute-start | bytes 12680 | tf_op jit(solution)/shard_map/ppermute | solution.py:21
  13.7 7.9 %copy-start.2 = (f32[128,128]{1,0:T(8,128)S(1)}, f32[128,128]{1,0:T(8,128)}, u32[]{:S(2)}) copy-start(f32[128,128]{1,0:T(8,128)} %param.4) | copy-start | bytes 196612
  13.7 5.7 %collective-permute-start.3 = (f32[4,132,2]{2,1,0:T(8,128)S(1)}, f32[4,132,2]{2,1,0:T(8,128)S(1)}, u32[]{:S(2)}, u32[]{:S(2)}) collective-permute-start(f32[4,132,2]{2,1,0:T(8,128)S(1)} %get-tuple-element.61), channel_id=1, source_target_pairs={{0,1},{1,2},{2,3},{3,4},{4,5},{5,6},{6,7},{7,0},{8,9},{9,10},{10,1... | collective-permute-start | bytes 12680 | tf_op jit(solution)/shard_map/ppermute | solution.py:18
  21.7 6.2 %collective-permute-start.5 = (f32[4,2,128]{2,1,0:T(2,128)S(1)}, f32[4,2,128]{2,1,0:T(2,128)S(1)}, u32[]{:S(2)}, u32[]{:S(2)}) collective-permute-start(f32[4,2,128]{2,1,0:T(2,128)S(1)} %get-tuple-element.70), channel_id=1, source_target_pairs={{0,8},{8,16},{16,24},{24,32},{32,40},{40,48},{48,56},{56,64},{64,7... | collective-permute-start | bytes 12296 | tf_op jit(solution)/shard_map/ppermute | solution.py:18
  21.8 6.1 %collective-permute-start.4 = (f32[4,2,128]{2,1,0:T(2,128)S(1)}, f32[4,2,128]{2,1,0:T(2,128)S(1)}, u32[]{:S(2)}, u32[]{:S(2)}) collective-permute-start(f32[4,2,128]{2,1,0:T(2,128)S(1)} %get-tuple-element.71), channel_id=1, source_target_pairs={{8,0},{16,8},{24,16},{32,24},{40,32},{48,40},{56,48},{64,56},{72,6... | collective-permute-start | bytes 12296 | tf_op jit(solution)/shard_map/ppermute | solution.py:21
  28.1 6.6 %collective-permute-start.6 = (f32[4,132,2]{2,1,0:T(8,128)S(1)}, f32[4,132,2]{2,1,0:T(8,128)S(1)}, u32[]{:S(2)}, u32[]{:S(2)}) collective-permute-start(f32[4,132,2]{2,1,0:T(8,128)S(1)} %get-tuple-element.58), channel_id=1, source_target_pairs={{1,0},{2,1},{3,2},{4,3},{5,4},{6,5},{7,6},{0,7},{9,8},{10,9},{11,1... | collective-permute-start | bytes 12680 | tf_op jit(solution)/shard_map/ppermute | solution.py:21
  32.0 3.5 %collective-permute-start.7 = (f32[4,132,2]{2,1,0:T(8,128)S(1)}, f32[4,132,2]{2,1,0:T(8,128)S(1)}, u32[]{:S(2)}, u32[]{:S(2)}) collective-permute-start(f32[4,132,2]{2,1,0:T(8,128)S(1)} %get-tuple-element.59), channel_id=1, source_target_pairs={{0,1},{1,2},{2,3},{3,4},{4,5},{5,6},{6,7},{7,0},{8,9},{9,10},{10,1... | collective-permute-start | bytes 12680 | tf_op jit(solution)/shard_map/ppermute | solution.py:18
  36.2 6.1 %collective-permute-start.9 = (f32[4,2,128]{2,1,0:T(2,128)S(1)}, f32[4,2,128]{2,1,0:T(2,128)S(1)}, u32[]{:S(2)}, u32[]{:S(2)}) collective-permute-start(f32[4,2,128]{2,1,0:T(2,128)S(1)} %get-tuple-element.68), channel_id=1, source_target_pairs={{0,8},{8,16},{16,24},{24,32},{32,40},{40,48},{48,56},{56,64},{64,7... | collective-permute-start | bytes 12296 | tf_op jit(solution)/shard_map/ppermute | solution.py:18
  36.3 6.0 %collective-permute-start.8 = (f32[4,2,128]{2,1,0:T(2,128)S(1)}, f32[4,2,128]{2,1,0:T(2,128)S(1)}, u32[]{:S(2)}, u32[]{:S(2)}) collective-permute-start(f32[4,2,128]{2,1,0:T(2,128)S(1)} %get-tuple-element.69), channel_id=1, source_target_pairs={{8,0},{16,8},{24,16},{32,24},{40,32},{48,40},{56,48},{64,56},{72,6... | collective-permute-start | bytes 12296 | tf_op jit(solution)/shard_map/ppermute | solution.py:21
  42.6 7.6 %collective-permute-start.10 = (f32[4,132,2]{2,1,0:T(8,128)S(1)}, f32[4,132,2]{2,1,0:T(8,128)S(1)}, u32[]{:S(2)}, u32[]{:S(2)}) collective-permute-start(f32[4,132,2]{2,1,0:T(8,128)S(1)} %get-tuple-element.56), channel_id=1, source_target_pairs={{1,0},{2,1},{3,2},{4,3},{5,4},{6,5},{7,6},{0,7},{9,8},{10,9},{11,1... | collective-permute-start | bytes 12680 | tf_op jit(solution)/shard_map/ppermute | solution.py:21
  47.1 3.5 %collective-permute-start.11 = (f32[4,132,2]{2,1,0:T(8,128)S(1)}, f32[4,132,2]{2,1,0:T(8,128)S(1)}, u32[]{:S(2)}, u32[]{:S(2)}) collective-permute-start(f32[4,132,2]{2,1,0:T(8,128)S(1)} %get-tuple-element.57), channel_id=1, source_target_pairs={{0,1},{1,2},{2,3},{3,4},{4,5},{5,6},{6,7},{7,0},{8,9},{9,10},{10,1... | collective-permute-start | bytes 12680 | tf_op jit(solution)/shard_map/ppermute | solution.py:18
  51.5 6.2 %collective-permute-start.13 = (f32[4,2,128]{2,1,0:T(2,128)S(1)}, f32[4,2,128]{2,1,0:T(2,128)S(1)}, u32[]{:S(2)}, u32[]{:S(2)}) collective-permute-start(f32[4,2,128]{2,1,0:T(2,128)S(1)} %get-tuple-element.66), channel_id=1, source_target_pairs={{0,8},{8,16},{16,24},{24,32},{32,40},{40,48},{48,56},{56,64},{64,7... | collective-permute-start | bytes 12296 | tf_op jit(solution)/shard_map/ppermute | solution.py:18
  51.5 6.1 %collective-permute-start.12 = (f32[4,2,128]{2,1,0:T(2,128)S(1)}, f32[4,2,128]{2,1,0:T(2,128)S(1)}, u32[]{:S(2)}, u32[]{:S(2)}) collective-permute-start(f32[4,2,128]{2,1,0:T(2,128)S(1)} %get-tuple-element.67), channel_id=1, source_target_pairs={{8,0},{16,8},{24,16},{32,24},{40,32},{48,40},{56,48},{64,56},{72,6... | collective-permute-start | bytes 12296 | tf_op jit(solution)/shard_map/ppermute | solution.py:21
  57.9 7.6 %collective-permute-start.14 = (f32[4,132,2]{2,1,0:T(8,128)S(1)}, f32[4,132,2]{2,1,0:T(8,128)S(1)}, u32[]{:S(2)}, u32[]{:S(2)}) collective-permute-start(f32[4,132,2]{2,1,0:T(8,128)S(1)} %get-tuple-element.54), channel_id=1, source_target_pairs={{1,0},{2,1},{3,2},{4,3},{5,4},{6,5},{7,6},{0,7},{9,8},{10,9},{11,1... | collective-permute-start | bytes 12680 | tf_op jit(solution)/shard_map/ppermute | solution.py:21
  62.5 3.5 %collective-permute-start.15 = (f32[4,132,2]{2,1,0:T(8,128)S(1)}, f32[4,132,2]{2,1,0:T(8,128)S(1)}, u32[]{:S(2)}, u32[]{:S(2)}) collective-permute-start(f32[4,132,2]{2,1,0:T(8,128)S(1)} %get-tuple-element.55), channel_id=1, source_target_pairs={{0,1},{1,2},{2,3},{3,4},{4,5},{5,6},{6,7},{7,0},{8,9},{9,10},{10,1... | collective-permute-start | bytes 12680 | tf_op jit(solution)/shard_map/ppermute | solution.py:18
  62.6 9.6 %copy-start.1 = (bf16[62,128,128]{2,1,0:T(8,128)(2,1)S(1)}, bf16[62,128,128]{2,1,0:T(8,128)(2,1)}, u32[]{:S(2)}) copy-start(bf16[62,128,128]{2,1,0:T(8,128)(2,1)} %param.5) | copy-start | bytes 6094852
  66.7 8.5 %collective-permute-start.17 = (f32[4,2,128]{2,1,0:T(2,128)S(1)}, f32[4,2,128]{2,1,0:T(2,128)S(1)}, u32[]{:S(2)}, u32[]{:S(2)}) collective-permute-start(f32[4,2,128]{2,1,0:T(2,128)S(1)} %get-tuple-element.64), channel_id=1, source_target_pairs={{0,8},{8,16},{16,24},{24,32},{32,40},{40,48},{48,56},{56,64},{64,7... | collective-permute-start | bytes 12296 | tf_op jit(solution)/shard_map/ppermute | solution.py:18
  66.8 8.4 %collective-permute-start.16 = (f32[4,2,128]{2,1,0:T(2,128)S(1)}, f32[4,2,128]{2,1,0:T(2,128)S(1)}, u32[]{:S(2)}, u32[]{:S(2)}) collective-permute-start(f32[4,2,128]{2,1,0:T(2,128)S(1)} %get-tuple-element.65), channel_id=1, source_target_pairs={{8,0},{16,8},{24,16},{32,24},{40,32},{48,40},{56,48},{64,56},{72,6... | collective-permute-start | bytes 12296 | tf_op jit(solution)/shard_map/ppermute | solution.py:21
  75.4 7.0 %collective-permute-start.18 = (f32[4,132,2]{2,1,0:T(8,128)S(1)}, f32[4,132,2]{2,1,0:T(8,128)S(1)}, u32[]{:S(2)}, u32[]{:S(2)}) collective-permute-start(f32[4,132,2]{2,1,0:T(8,128)S(1)} %get-tuple-element.52), channel_id=1, source_target_pairs={{1,0},{2,1},{3,2},{4,3},{5,4},{6,5},{7,6},{0,7},{9,8},{10,9},{11,1... | collective-permute-start | bytes 12680 | tf_op jit(solution)/shard_map/ppermute | solution.py:21
  79.4 3.5 %collective-permute-start.19 = (f32[4,132,2]{2,1,0:T(8,128)S(1)}, f32[4,132,2]{2,1,0:T(8,128)S(1)}, u32[]{:S(2)}, u32[]{:S(2)}) collective-permute-start(f32[4,132,2]{2,1,0:T(8,128)S(1)} %get-tuple-element.53), channel_id=1, source_target_pairs={{0,1},{1,2},{2,3},{3,4},{4,5},{5,6},{6,7},{7,0},{8,9},{9,10},{10,1... | collective-permute-start | bytes 12680 | tf_op jit(solution)/shard_map/ppermute | solution.py:18
  83.6 5.9 %collective-permute-start.21 = (f32[4,2,128]{2,1,0:T(2,128)S(1)}, f32[4,2,128]{2,1,0:T(2,128)S(1)}, u32[]{:S(2)}, u32[]{:S(2)}) collective-permute-start(f32[4,2,128]{2,1,0:T(2,128)S(1)} %get-tuple-element.62), channel_id=1, source_target_pairs={{0,8},{8,16},{16,24},{24,32},{32,40},{40,48},{48,56},{56,64},{64,7... | collective-permute-start | bytes 12296 | tf_op jit(solution)/shard_map/ppermute | solution.py:18
  83.7 5.8 %collective-permute-start.20 = (f32[4,2,128]{2,1,0:T(2,128)S(1)}, f32[4,2,128]{2,1,0:T(2,128)S(1)}, u32[]{:S(2)}, u32[]{:S(2)}) collective-permute-start(f32[4,2,128]{2,1,0:T(2,128)S(1)} %get-tuple-element.63), channel_id=1, source_target_pairs={{8,0},{16,8},{24,16},{32,24},{40,32},{48,40},{56,48},{64,56},{72,6... | collective-permute-start | bytes 12296 | tf_op jit(solution)/shard_map/ppermute | solution.py:21
  89.7 7.9 %collective-permute-start.22 = (f32[4,132,2]{2,1,0:T(8,128)S(1)}, f32[4,132,2]{2,1,0:T(8,128)S(1)}, u32[]{:S(2)}, u32[]{:S(2)}) collective-permute-start(f32[4,132,2]{2,1,0:T(8,128)S(1)} %get-tuple-element.50), channel_id=1, source_target_pairs={{1,0},{2,1},{3,2},{4,3},{5,4},{6,5},{7,6},{0,7},{9,8},{10,9},{11,1... | collective-permute-start | bytes 12680 | tf_op jit(solution)/shard_map/ppermute | solution.py:21
  94.5 3.5 %collective-permute-start.23 = (f32[4,132,2]{2,1,0:T(8,128)S(1)}, f32[4,132,2]{2,1,0:T(8,128)S(1)}, u32[]{:S(2)}, u32[]{:S(2)}) collective-permute-start(f32[4,132,2]{2,1,0:T(8,128)S(1)} %get-tuple-element.51), channel_id=1, source_target_pairs={{0,1},{1,2},{2,3},{3,4},{4,5},{5,6},{6,7},{7,0},{8,9},{9,10},{10,1... | collective-permute-start | bytes 12680 | tf_op jit(solution)/shard_map/ppermute | solution.py:18
  98.8 0.8 copy-start.3
where the time goes:
time: 197 us
  blocking collectives  78.8 us (40%)
  starting transfers between devices  59.6 us (30%)
  waiting for transfers between devices  25.9 us (13%)
  other arithmetic  19.7 us (10%)
  local copies, waits for them, and re-layouts  9.39 us (5%)
  matrix products  2.72 us (1%)
    psum x1, blocking collectives, body(): gram = lax.psum(local_gram, ('gx', 'gy'))  78.8 us
    ppermute x12, starting transfers between devices, padded_2(): lax.ppermute(lax.slice_in_dim(block, 0, width, axis=dim), axis, backward)  55.4 us
    ppermute x12, waiting for transfers between devices, padded_2(): lax.ppermute(lax.slice_in_dim(block, 0, width, axis=dim), axis, backward)  18.6 us
    unnamed x14, local copies, waits for them, and re-layouts  7.46 us
    ppermute x12, waiting for transfers between devices, padded_2(): lax.ppermute(lax.slice_in_dim(block, block.shape[dim] - width, None, axis...  7.3 us
    another operation x3, other arithmetic, body(): lower_factor = jnp.linalg.cholesky(gram)  6.52 us
    another operation x2, other arithmetic, body(): jax.scipy.linalg.solve_triangular(lower_factor, identity_matrix, lower=True)  5.55 us
    div x6, other arithmetic, derivative_y(): return (8.0 * (ahead_one - behind_one) - (ahead_two - behind_two)) / 12.0  4.75 us
  transfers between devices with their start and end apart: 24, of which 16 were waited for; matrix products, arithmetic and copies ran while one was open for 2% of the time, Pallas kernels for 0%

commit v1 on v0

--- a/solution.py
+++ b/solution.py
@@ -81,7 +81,7 @@
         )
         / cell_total
     )
-    gram = lax.psum(local_gram, ("gx", "gy"))
+    gram = jnp.sum(lax.all_gather(local_gram, ("gx", "gy")), 0)
     lower_factor = jnp.linalg.cholesky(gram)
     identity_matrix = jnp.eye(mode_count, dtype=jnp.float32)
     inverse = jax.scipy.linalg.solve_triangular(lower_factor, identity_matrix, lower=True)

time: 197 us -> 253 us (1.28)
  waiting for transfers between devices: 25.9 us -> 159 us
  blocking collectives: 78.8 us -> 0 us
  starting transfers between devices: 59.6 us -> 43 us
  between operations: 1.17 us -> 14.5 us
  other arithmetic: 19.7 us -> 23.8 us
    all_gather x0 -> x1, waiting for transfers between devices: none -> 111 us  [body(): gram = jnp.sum(lax.all_gather(local_gram, ('gx', 'gy')), 0)]
    psum x1 -> x0, blocking collectives: 78.8 us -> none  [body(): gram = lax.psum(local_gram, ('gx', 'gy'))]
    ppermute x12, starting transfers between devices: 55.4 us -> 34.5 us  [padded_2(): lax.ppermute(lax.slice_in_dim(block, 0, width, axis=dim), axis, backward)]
    ppermute x12, waiting for transfers between devices: 7.3 us -> 24.2 us  [padded_2(): lax.ppermute(lax.slice_in_dim(block, block.shape[dim] - width, None, axis...]
    ppermute x12, waiting for transfers between devices: 18.6 us -> 23.7 us  [padded_2(): lax.ppermute(lax.slice_in_dim(block, 0, width, axis=dim), axis, backward)]
    ppermute x12, starting transfers between devices: 4.12 us -> 8.5 us  [padded_2(): lax.ppermute(lax.slice_in_dim(block, block.shape[dim] - width, None, axis...]
    reduce_sum x0 -> x1, other arithmetic: none -> 4.01 us  [body(): gram = jnp.sum(lax.all_gather(local_gram, ('gx', 'gy')), 0)]
  transfers between devices with their start and end apart: 24 -> 25, of which waited for: 16 -> 23; matrix products, arithmetic and copies ran while one was open for 2% -> 1% of each run, Pallas kernels for 0% -> 0%
where the time goes in v1:
time: 253 us
  waiting for transfers between devices  159 us (63%)
  starting transfers between devices  43 us (17%)
  other arithmetic  23.8 us (9%)
  between operations  14.5 us (6%)
  local copies, waits for them, and re-layouts  9.28 us (4%)
  matrix products  3.33 us (1%)
    all_gather x1, waiting for transfers between devices, body(): gram = jnp.sum(lax.all_gather(local_gram, ('gx', 'gy')), 0)  111 us
    ppermute x12, starting transfers between devices, padded_2(): lax.ppermute(lax.slice_in_dim(block, 0, width, axis=dim), axis, backward)  34.5 us
    ppermute x12, waiting for transfers between devices, padded_2(): lax.ppermute(lax.slice_in_dim(block, block.shape[dim] - width, None, axis...  24.2 us
    ppermute x12, waiting for transfers between devices, padded_2(): lax.ppermute(lax.slice_in_dim(block, 0, width, axis=dim), axis, backward)  23.7 us
    ppermute x12, starting transfers between devices, padded_2(): lax.ppermute(lax.slice_in_dim(block, block.shape[dim] - width, None, axis...  8.5 us
    unnamed x14, local copies, waits for them, and re-layouts  7.36 us
    another operation x3, other arithmetic, body(): lower_factor = jnp.linalg.cholesky(gram)  6.52 us
    another operation x2, other arithmetic, body(): jax.scipy.linalg.solve_triangular(lower_factor, identity_matrix, lower=True)  5.55 us
  transfers between devices with their start and end apart: 25, of which 23 were waited for; matrix products, arithmetic and copies ran while one was open for 1% of the time, Pallas kernels for 0%

profile of v1, /device:TPU:1, one launch (start us, length us, event | category | flops | bytes accessed | tf_op | source)
XLA Modules:
  0.0 252.8 jit_solution(4214853314148689613)
XLA Ops:
  7.2 0.8 fusion.139
  8.0 8.6 %collective-permute-start = (f32[4,2,128]{2,1,0:T(2,128)S(1)}, f32[4,2,128]{2,1,0:T(2,128)S(1)}, u32[]{:S(2)}, u32[]{:S(2)}) collective-permute-start(f32[4,2,128]{2,1,0:T(2,128)S(1)} %get-tuple-element.76), channel_id=1, source_target_pairs={{8,0},{16,8},{24,16},{32,24},{40,32},{48,40},{56,48},{64,56},{72,6... | collective-permute-start | bytes 12296 | tf_op jit(solution)/shard_map/ppermute | solution.py:21
  16.6 0.8 collective-permute-done
  17.4 5.0 %collective-permute-done.1 = f32[4,2,128]{2,1,0:T(2,128)S(1)} collective-permute-done((f32[4,2,128]{2,1,0:T(2,128)S(1)}, f32[4,2,128]{2,1,0:T(2,128)S(1)}, u32[]{:S(2)}, u32[]{:S(2)}) %collective-permute-start.1) | collective-permute-done | bytes 4128 | tf_op jit(solution)/shard_map/ppermute | solution.py:18
  22.4 1.0 pad_maximum_fusion
  23.5 2.1 collective-permute-start.2
  25.6 1.2 collective-permute-start.3
  26.8 4.5 %collective-permute-done.2 = f32[4,132,2]{2,1,0:T(8,128)S(1)} collective-permute-done((f32[4,132,2]{2,1,0:T(8,128)S(1)}, f32[4,132,2]{2,1,0:T(8,128)S(1)}, u32[]{:S(2)}, u32[]{:S(2)}) %collective-permute-start.2) | collective-permute-done | bytes 4256 | tf_op jit(solution)/shard_map/ppermute | solution.py:21
  31.3 2.1 broadcast_multiply_fusion.10
  33.8 1.5 collective-permute-start.5
  35.3 1.0 collective-permute-done.4
  36.3 3.4 %collective-permute-done.5 = f32[4,2,128]{2,1,0:T(2,128)S(1)} collective-permute-done((f32[4,2,128]{2,1,0:T(2,128)S(1)}, f32[4,2,128]{2,1,0:T(2,128)S(1)}, u32[]{:S(2)}, u32[]{:S(2)}) %collective-permute-start.5) | collective-permute-done | bytes 4128 | tf_op jit(solution)/shard_map/ppermute | solution.py:18
  39.8 3.8 %collective-permute-start.6 = (f32[4,132,2]{2,1,0:T(8,128)S(1)}, f32[4,132,2]{2,1,0:T(8,128)S(1)}, u32[]{:S(2)}, u32[]{:S(2)}) collective-permute-start(f32[4,132,2]{2,1,0:T(8,128)S(1)} %get-tuple-element.60), channel_id=1, source_target_pairs={{1,0},{2,1},{3,2},{4,3},{5,4},{6,5},{7,6},{0,7},{9,8},{10,9},{11,1... | collective-permute-start | bytes 12680 | tf_op jit(solution)/shard_map/ppermute | solution.py:21
  43.8 2.9 %collective-permute-done.6 = f32[4,132,2]{2,1,0:T(8,128)S(1)} collective-permute-done((f32[4,132,2]{2,1,0:T(8,128)S(1)}, f32[4,132,2]{2,1,0:T(8,128)S(1)}, u32[]{:S(2)}, u32[]{:S(2)}) %collective-permute-start.6) | collective-permute-done | bytes 4256 | tf_op jit(solution)/shard_map/ppermute | solution.py:21
  47.2 0.6 broadcast_multiply_fusion.8
  48.0 1.5 collective-permute-start.9
  49.5 1.0 collective-permute-done.8
  50.5 3.4 %collective-permute-done.9 = f32[4,2,128]{2,1,0:T(2,128)S(1)} collective-permute-done((f32[4,2,128]{2,1,0:T(2,128)S(1)}, f32[4,2,128]{2,1,0:T(2,128)S(1)}, u32[]{:S(2)}, u32[]{:S(2)}) %collective-permute-start.9) | collective-permute-done | bytes 4128 | tf_op jit(solution)/shard_map/ppermute | solution.py:18
  54.1 4.9 %collective-permute-start.10 = (f32[4,132,2]{2,1,0:T(8,128)S(1)}, f32[4,132,2]{2,1,0:T(8,128)S(1)}, u32[]{:S(2)}, u32[]{:S(2)}) collective-permute-start(f32[4,132,2]{2,1,0:T(8,128)S(1)} %get-tuple-element.58), channel_id=1, source_target_pairs={{1,0},{2,1},{3,2},{4,3},{5,4},{6,5},{7,6},{0,7},{9,8},{10,9},{11,1... | collective-permute-start | bytes 12680 | tf_op jit(solution)/shard_map/ppermute | solution.py:21
  59.1 2.9 %collective-permute-done.10 = f32[4,132,2]{2,1,0:T(8,128)S(1)} collective-permute-done((f32[4,132,2]{2,1,0:T(8,128)S(1)}, f32[4,132,2]{2,1,0:T(8,128)S(1)}, u32[]{:S(2)}, u32[]{:S(2)}) %collective-permute-start.10) | collective-permute-done | bytes 4256 | tf_op jit(solution)/shard_map/ppermute | solution.py:21
  62.4 0.6 broadcast_multiply_fusion.6
  63.3 1.5 collective-permute-start.13
  64.8 1.0 collective-permute-done.12
  65.8 3.4 %collective-permute-done.13 = f32[4,2,128]{2,1,0:T(2,128)S(1)} collective-permute-done((f32[4,2,128]{2,1,0:T(2,128)S(1)}, f32[4,2,128]{2,1,0:T(2,128)S(1)}, u32[]{:S(2)}, u32[]{:S(2)}) %collective-permute-start.13) | collective-permute-done | bytes 4128 | tf_op jit(solution)/shard_map/ppermute | solution.py:18
  69.3 4.9 %collective-permute-start.14 = (f32[4,132,2]{2,1,0:T(8,128)S(1)}, f32[4,132,2]{2,1,0:T(8,128)S(1)}, u32[]{:S(2)}, u32[]{:S(2)}) collective-permute-start(f32[4,132,2]{2,1,0:T(8,128)S(1)} %get-tuple-element.56), channel_id=1, source_target_pairs={{1,0},{2,1},{3,2},{4,3},{5,4},{6,5},{7,6},{0,7},{9,8},{10,9},{11,1... | collective-permute-start | bytes 12680 | tf_op jit(solution)/shard_map/ppermute | solution.py:21
  74.3 2.9 %collective-permute-done.14 = f32[4,132,2]{2,1,0:T(8,128)S(1)} collective-permute-done((f32[4,132,2]{2,1,0:T(8,128)S(1)}, f32[4,132,2]{2,1,0:T(8,128)S(1)}, u32[]{:S(2)}, u32[]{:S(2)}) %collective-permute-start.14) | collective-permute-done | bytes 4256 | tf_op jit(solution)/shard_map/ppermute | solution.py:21
  78.5 1.5 collective-permute-start.17
  80.0 1.0 collective-permute-done.16
  81.0 3.5 %collective-permute-done.17 = f32[4,2,128]{2,1,0:T(2,128)S(1)} collective-permute-done((f32[4,2,128]{2,1,0:T(2,128)S(1)}, f32[4,2,128]{2,1,0:T(2,128)S(1)}, u32[]{:S(2)}, u32[]{:S(2)}) %collective-permute-start.17) | collective-permute-done | bytes 4128 | tf_op jit(solution)/shard_map/ppermute | solution.py:18
  84.8 4.9 %collective-permute-start.18 = (f32[4,132,2]{2,1,0:T(8,128)S(1)}, f32[4,132,2]{2,1,0:T(8,128)S(1)}, u32[]{:S(2)}, u32[]{:S(2)}) collective-permute-start(f32[4,132,2]{2,1,0:T(8,128)S(1)} %get-tuple-element.54), channel_id=1, source_target_pairs={{1,0},{2,1},{3,2},{4,3},{5,4},{6,5},{7,6},{0,7},{9,8},{10,9},{11,1... | collective-permute-start | bytes 12680 | tf_op jit(solution)/shard_map/ppermute | solution.py:21
  89.8 2.9 %collective-permute-done.18 = f32[4,132,2]{2,1,0:T(8,128)S(1)} collective-permute-done((f32[4,132,2]{2,1,0:T(8,128)S(1)}, f32[4,132,2]{2,1,0:T(8,128)S(1)}, u32[]{:S(2)}, u32[]{:S(2)}) %collective-permute-start.18) | collective-permute-done | bytes 4256 | tf_op jit(solution)/shard_map/ppermute | solution.py:21
  93.1 0.6 broadcast_multiply_fusion.2
  94.0 1.5 collective-permute-start.21
  95.4 1.3 copy.94
  96.8 3.0 %collective-permute-done.21 = f32[4,2,128]{2,1,0:T(2,128)S(1)} collective-permute-done((f32[4,2,128]{2,1,0:T(2,128)S(1)}, f32[4,2,128]{2,1,0:T(2,128)S(1)}, u32[]{:S(2)}, u32[]{:S(2)}) %collective-permute-start.21) | collective-permute-done | bytes 4128 | tf_op jit(solution)/shard_map/ppermute | solution.py:18
  100.0 4.9 %collective-permute-start.22 = (f32[4,132,2]{2,1,0:T(8,128)S(1)}, f32[4,132,2]{2,1,0:T(8,128)S(1)}, u32[]{:S(2)}, u32[]{:S(2)}) collective-permute-start(f32[4,132,2]{2,1,0:T(8,128)S(1)} %get-tuple-element.52), channel_id=1, source_target_pairs={{1,0},{2,1},{3,2},{4,3},{5,4},{6,5},{7,6},{0,7},{9,8},{10,9},{11,1... | collective-permute-start | bytes 12680 | tf_op jit(solution)/shard_map/ppermute | solution.py:21
  105.0 2.9 %collective-permute-done.22 = f32[4,132,2]{2,1,0:T(8,128)S(1)} collective-permute-done((f32[4,132,2]{2,1,0:T(8,128)S(1)}, f32[4,132,2]{2,1,0:T(8,128)S(1)}, u32[]{:S(2)}, u32[]{:S(2)}) %collective-permute-start.22) | collective-permute-done | bytes 4256 | tf_op jit(solution)/shard_map/ppermute | solution.py:21
  108.4 0.6 broadcast_multiply_fusion
  109.2 1.3 fusion.12
  110.8 1.4 copy.101
  112.3 111.0 %all-gather.3.cloned.1.call-done = f32[16384,64]{1,0:T(8,128)} async-done(((f32[64,64]{1,0:T(8,128)}), f32[16384,64]{1,0:T(8,128)}) %all-gather.3.cloned.1.call-update) | async-done | bytes 4194320 | tf_op jit(solution)/shard_map/all_gather | solution.py:84
  223.3 4.0 %reduce_sum.9 = f32[64,64]{1,0:T(8,128)S(1)} reduce(f32[256,64,64]{2,1,0:T(8,128)} %bitcast.121, f32[]{:T(128)} %constant.85.clone.1), dimensions={0}, to_apply=%region_0.0 | reduce | flops 1044480 | bytes 4210692 | tf_op jit(solution)/shard_map/reduce_sum | solution.py:84
  227.4 5.8 %cholesky.17 = f32[64,64]{1,0:T(8,128)S(1)} custom-call(f32[64,64]{1,0:T(8,128)S(1)} %fusion.114), custom_call_target="Cholesky" | custom-call | tf_op jit(solution)/shard_map/jit(cholesky)/cholesky | solution.py:85
  233.3 0.6 compare_reduce_fusion
  233.9 0.7 fusion.112
  234.6 4.9 %custom-call.7 = f32[1,64,64]{1,2,0:T(8,128)S(1)} custom-call(f32[1,64,64]{2,1,0:T(8,128)S(1)} %fusion.112), custom_call_target="InvertDiagBlocksLowerTriangular" | custom-call | tf_op jit(solution)/shard_map/jit(_solve_triangular)/triangular_solve | solution.py:87
  239.7 1.8 fusion
  241.5 4.4 %copy.99 = f32[64,128,128]{2,1,0:T(8,128)} copy(f32[64,128,128]{2,0,1:T(8,128)S(1)} %fusion) | data formatting | bytes 8388608
  (88 shorter events, 7.0 us)
Async XLA Ops:
  7.2 26.2 %copy-start = (f32[4,128,128]{2,1,0:T(8,128)S(1)}, f32[4,128,128]{2,1,0:T(8,128)}, u32[]{:S(2)}) copy-start(f32[4,128,128]{2,1,0:T(8,128)} %param.3) | copy-start | bytes 786436
  7.2 216.1 %all-gather.3.cloned.1.call-start = ((), (), s32[]{:S(2)}) async-start(), calls=%async_computation | async-start | bytes 8421376 | tf_op jit(solution)/shard_map/all_gather | solution.py:84
  8.0 9.4 %collective-permute-start = (f32[4,2,128]{2,1,0:T(2,128)S(1)}, f32[4,2,128]{2,1,0:T(2,128)S(1)}, u32[]{:S(2)}, u32[]{:S(2)}) collective-permute-start(f32[4,2,128]{2,1,0:T(2,128)S(1)} %get-tuple-element.76), channel_id=1, source_target_pairs={{8,0},{16,8},{24,16},{32,24},{40,32},{48,40},{56,48},{64,56},{72,6... | collective-permute-start | bytes 12296 | tf_op jit(solution)/shard_map/ppermute | solution.py:21
  16.6 5.8 %collective-permute-start.1 = (f32[4,2,128]{2,1,0:T(2,128)S(1)}, f32[4,2,128]{2,1,0:T(2,128)S(1)}, u32[]{:S(2)}, u32[]{:S(2)}) collective-permute-start(f32[4,2,128]{2,1,0:T(2,128)S(1)} %get-tuple-element.75), channel_id=1, source_target_pairs={{0,8},{8,16},{16,24},{24,32},{32,40},{40,48},{48,56},{56,64},{64,7... | collective-permute-start | bytes 12296 | tf_op jit(solution)/shard_map/ppermute | solution.py:18
  23.5 7.8 %collective-permute-start.2 = (f32[4,132,2]{2,1,0:T(8,128)S(1)}, f32[4,132,2]{2,1,0:T(8,128)S(1)}, u32[]{:S(2)}, u32[]{:S(2)}) collective-permute-start(f32[4,132,2]{2,1,0:T(8,128)S(1)} %get-tuple-element.62), channel_id=1, source_target_pairs={{1,0},{2,1},{3,2},{4,3},{5,4},{6,5},{7,6},{0,7},{9,8},{10,9},{11,1... | collective-permute-start | bytes 12680 | tf_op jit(solution)/shard_map/ppermute | solution.py:21
  25.6 8.0 %copy-start.2 = (f32[128,128]{1,0:T(8,128)S(1)}, f32[128,128]{1,0:T(8,128)}, u32[]{:S(2)}) copy-start(f32[128,128]{1,0:T(8,128)} %param.4) | copy-start | bytes 196612
  25.6 5.7 %collective-permute-start.3 = (f32[4,132,2]{2,1,0:T(8,128)S(1)}, f32[4,132,2]{2,1,0:T(8,128)S(1)}, u32[]{:S(2)}, u32[]{:S(2)}) collective-permute-start(f32[4,132,2]{2,1,0:T(8,128)S(1)} %get-tuple-element.63), channel_id=1, source_target_pairs={{0,1},{1,2},{2,3},{3,4},{4,5},{5,6},{6,7},{7,0},{8,9},{9,10},{10,1... | collective-permute-start | bytes 12680 | tf_op jit(solution)/shard_map/ppermute | solution.py:18
  33.7 2.5 %collective-permute-start.4 = (f32[4,2,128]{2,1,0:T(2,128)S(1)}, f32[4,2,128]{2,1,0:T(2,128)S(1)}, u32[]{:S(2)}, u32[]{:S(2)}) collective-permute-start(f32[4,2,128]{2,1,0:T(2,128)S(1)} %get-tuple-element.73), channel_id=1, source_target_pairs={{8,0},{16,8},{24,16},{32,24},{40,32},{48,40},{56,48},{64,56},{72,6... | collective-permute-start | bytes 12296 | tf_op jit(solution)/shard_map/ppermute | solution.py:21
  33.8 5.9 %collective-permute-start.5 = (f32[4,2,128]{2,1,0:T(2,128)S(1)}, f32[4,2,128]{2,1,0:T(2,128)S(1)}, u32[]{:S(2)}, u32[]{:S(2)}) collective-permute-start(f32[4,2,128]{2,1,0:T(2,128)S(1)} %get-tuple-element.72), channel_id=1, source_target_pairs={{0,8},{8,16},{16,24},{24,32},{32,40},{40,48},{48,56},{56,64},{64,7... | collective-permute-start | bytes 12296 | tf_op jit(solution)/shard_map/ppermute | solution.py:18
  39.8 6.9 %collective-permute-start.6 = (f32[4,132,2]{2,1,0:T(8,128)S(1)}, f32[4,132,2]{2,1,0:T(8,128)S(1)}, u32[]{:S(2)}, u32[]{:S(2)}) collective-permute-start(f32[4,132,2]{2,1,0:T(8,128)S(1)} %get-tuple-element.60), channel_id=1, source_target_pairs={{1,0},{2,1},{3,2},{4,3},{5,4},{6,5},{7,6},{0,7},{9,8},{10,9},{11,1... | collective-permute-start | bytes 12680 | tf_op jit(solution)/shard_map/ppermute | solution.py:21
  43.7 3.5 %collective-permute-start.7 = (f32[4,132,2]{2,1,0:T(8,128)S(1)}, f32[4,132,2]{2,1,0:T(8,128)S(1)}, u32[]{:S(2)}, u32[]{:S(2)}) collective-permute-start(f32[4,132,2]{2,1,0:T(8,128)S(1)} %get-tuple-element.61), channel_id=1, source_target_pairs={{0,1},{1,2},{2,3},{3,4},{4,5},{5,6},{6,7},{7,0},{8,9},{9,10},{10,1... | collective-permute-start | bytes 12680 | tf_op jit(solution)/shard_map/ppermute | solution.py:18
  47.9 2.6 %collective-permute-start.8 = (f32[4,2,128]{2,1,0:T(2,128)S(1)}, f32[4,2,128]{2,1,0:T(2,128)S(1)}, u32[]{:S(2)}, u32[]{:S(2)}) collective-permute-start(f32[4,2,128]{2,1,0:T(2,128)S(1)} %get-tuple-element.71), channel_id=1, source_target_pairs={{8,0},{16,8},{24,16},{32,24},{40,32},{48,40},{56,48},{64,56},{72,6... | collective-permute-start | bytes 12296 | tf_op jit(solution)/shard_map/ppermute | solution.py:21
  48.0 5.9 %collective-permute-start.9 = (f32[4,2,128]{2,1,0:T(2,128)S(1)}, f32[4,2,128]{2,1,0:T(2,128)S(1)}, u32[]{:S(2)}, u32[]{:S(2)}) collective-permute-start(f32[4,2,128]{2,1,0:T(2,128)S(1)} %get-tuple-element.70), channel_id=1, source_target_pairs={{0,8},{8,16},{16,24},{24,32},{32,40},{40,48},{48,56},{56,64},{64,7... | collective-permute-start | bytes 12296 | tf_op jit(solution)/shard_map/ppermute | solution.py:18
  54.1 7.9 %collective-permute-start.10 = (f32[4,132,2]{2,1,0:T(8,128)S(1)}, f32[4,132,2]{2,1,0:T(8,128)S(1)}, u32[]{:S(2)}, u32[]{:S(2)}) collective-permute-start(f32[4,132,2]{2,1,0:T(8,128)S(1)} %get-tuple-element.58), channel_id=1, source_target_pairs={{1,0},{2,1},{3,2},{4,3},{5,4},{6,5},{7,6},{0,7},{9,8},{10,9},{11,1... | collective-permute-start | bytes 12680 | tf_op jit(solution)/shard_map/ppermute | solution.py:21
  58.9 3.5 %collective-permute-start.11 = (f32[4,132,2]{2,1,0:T(8,128)S(1)}, f32[4,132,2]{2,1,0:T(8,128)S(1)}, u32[]{:S(2)}, u32[]{:S(2)}) collective-permute-start(f32[4,132,2]{2,1,0:T(8,128)S(1)} %get-tuple-element.59), channel_id=1, source_target_pairs={{0,1},{1,2},{2,3},{3,4},{4,5},{5,6},{6,7},{7,0},{8,9},{9,10},{10,1... | collective-permute-start | bytes 12680 | tf_op jit(solution)/shard_map/ppermute | solution.py:18
  63.2 2.5 %collective-permute-start.12 = (f32[4,2,128]{2,1,0:T(2,128)S(1)}, f32[4,2,128]{2,1,0:T(2,128)S(1)}, u32[]{:S(2)}, u32[]{:S(2)}) collective-permute-start(f32[4,2,128]{2,1,0:T(2,128)S(1)} %get-tuple-element.69), channel_id=1, source_target_pairs={{8,0},{16,8},{24,16},{32,24},{40,32},{48,40},{56,48},{64,56},{72,6... | collective-permute-start | bytes 12296 | tf_op jit(solution)/shard_map/ppermute | solution.py:21
  63.3 5.9 %collective-permute-start.13 = (f32[4,2,128]{2,1,0:T(2,128)S(1)}, f32[4,2,128]{2,1,0:T(2,128)S(1)}, u32[]{:S(2)}, u32[]{:S(2)}) collective-permute-start(f32[4,2,128]{2,1,0:T(2,128)S(1)} %get-tuple-element.68), channel_id=1, source_target_pairs={{0,8},{8,16},{16,24},{24,32},{32,40},{40,48},{48,56},{56,64},{64,7... | collective-permute-start | bytes 12296 | tf_op jit(solution)/shard_map/ppermute | solution.py:18
  69.3 7.9 %collective-permute-start.14 = (f32[4,132,2]{2,1,0:T(8,128)S(1)}, f32[4,132,2]{2,1,0:T(8,128)S(1)}, u32[]{:S(2)}, u32[]{:S(2)}) collective-permute-start(f32[4,132,2]{2,1,0:T(8,128)S(1)} %get-tuple-element.56), channel_id=1, source_target_pairs={{1,0},{2,1},{3,2},{4,3},{5,4},{6,5},{7,6},{0,7},{9,8},{10,9},{11,1... | collective-permute-start | bytes 12680 | tf_op jit(solution)/shard_map/ppermute | solution.py:21
  74.2 3.5 %collective-permute-start.15 = (f32[4,132,2]{2,1,0:T(8,128)S(1)}, f32[4,132,2]{2,1,0:T(8,128)S(1)}, u32[]{:S(2)}, u32[]{:S(2)}) collective-permute-start(f32[4,132,2]{2,1,0:T(8,128)S(1)} %get-tuple-element.57), channel_id=1, source_target_pairs={{0,1},{1,2},{2,3},{3,4},{4,5},{5,6},{6,7},{7,0},{8,9},{9,10},{10,1... | collective-permute-start | bytes 12680 | tf_op jit(solution)/shard_map/ppermute | solution.py:18
  78.5 2.6 %collective-permute-start.16 = (f32[4,2,128]{2,1,0:T(2,128)S(1)}, f32[4,2,128]{2,1,0:T(2,128)S(1)}, u32[]{:S(2)}, u32[]{:S(2)}) collective-permute-start(f32[4,2,128]{2,1,0:T(2,128)S(1)} %get-tuple-element.67), channel_id=1, source_target_pairs={{8,0},{16,8},{24,16},{32,24},{40,32},{48,40},{56,48},{64,56},{72,6... | collective-permute-start | bytes 12296 | tf_op jit(solution)/shard_map/ppermute | solution.py:21
  78.5 6.0 %collective-permute-start.17 = (f32[4,2,128]{2,1,0:T(2,128)S(1)}, f32[4,2,128]{2,1,0:T(2,128)S(1)}, u32[]{:S(2)}, u32[]{:S(2)}) collective-permute-start(f32[4,2,128]{2,1,0:T(2,128)S(1)} %get-tuple-element.66), channel_id=1, source_target_pairs={{0,8},{8,16},{16,24},{24,32},{32,40},{40,48},{48,56},{56,64},{64,7... | collective-permute-start | bytes 12296 | tf_op jit(solution)/shard_map/ppermute | solution.py:18
  84.8 7.9 %collective-permute-start.18 = (f32[4,132,2]{2,1,0:T(8,128)S(1)}, f32[4,132,2]{2,1,0:T(8,128)S(1)}, u32[]{:S(2)}, u32[]{:S(2)}) collective-permute-start(f32[4,132,2]{2,1,0:T(8,128)S(1)} %get-tuple-element.54), channel_id=1, source_target_pairs={{1,0},{2,1},{3,2},{4,3},{5,4},{6,5},{7,6},{0,7},{9,8},{10,9},{11,1... | collective-permute-start | bytes 12680 | tf_op jit(solution)/shard_map/ppermute | solution.py:21
  89.6 3.5 %collective-permute-start.19 = (f32[4,132,2]{2,1,0:T(8,128)S(1)}, f32[4,132,2]{2,1,0:T(8,128)S(1)}, u32[]{:S(2)}, u32[]{:S(2)}) collective-permute-start(f32[4,132,2]{2,1,0:T(8,128)S(1)} %get-tuple-element.55), channel_id=1, source_target_pairs={{0,1},{1,2},{2,3},{3,4},{4,5},{5,6},{6,7},{7,0},{8,9},{9,10},{10,1... | collective-permute-start | bytes 12680 | tf_op jit(solution)/shard_map/ppermute | solution.py:18
  89.8 5.7 %copy-start.1 = (bf16[62,128,128]{2,1,0:T(8,128)(2,1)S(1)}, bf16[62,128,128]{2,1,0:T(8,128)(2,1)}, u32[]{:S(2)}) copy-start(bf16[62,128,128]{2,1,0:T(8,128)(2,1)} %param.5) | copy-start | bytes 6094852
  93.9 2.9 %collective-permute-start.20 = (f32[4,2,128]{2,1,0:T(2,128)S(1)}, f32[4,2,128]{2,1,0:T(2,128)S(1)}, u32[]{:S(2)}, u32[]{:S(2)}) collective-permute-start(f32[4,2,128]{2,1,0:T(2,128)S(1)} %get-tuple-element.65), channel_id=1, source_target_pairs={{8,0},{16,8},{24,16},{32,24},{40,32},{48,40},{56,48},{64,56},{72,6... | collective-permute-start | bytes 12296 | tf_op jit(solution)/shard_map/ppermute | solution.py:21
  94.0 5.9 %collective-permute-start.21 = (f32[4,2,128]{2,1,0:T(2,128)S(1)}, f32[4,2,128]{2,1,0:T(2,128)S(1)}, u32[]{:S(2)}, u32[]{:S(2)}) collective-permute-start(f32[4,2,128]{2,1,0:T(2,128)S(1)} %get-tuple-element.64), channel_id=1, source_target_pairs={{0,8},{8,16},{16,24},{24,32},{32,40},{40,48},{48,56},{56,64},{64,7... | collective-permute-start | bytes 12296 | tf_op jit(solution)/shard_map/ppermute | solution.py:18
  100.0 7.9 %collective-permute-start.22 = (f32[4,132,2]{2,1,0:T(8,128)S(1)}, f32[4,132,2]{2,1,0:T(8,128)S(1)}, u32[]{:S(2)}, u32[]{:S(2)}) collective-permute-start(f32[4,132,2]{2,1,0:T(8,128)S(1)} %get-tuple-element.52), channel_id=1, source_target_pairs={{1,0},{2,1},{3,2},{4,3},{5,4},{6,5},{7,6},{0,7},{9,8},{10,9},{11,1... | collective-permute-start | bytes 12680 | tf_op jit(solution)/shard_map/ppermute | solution.py:21
  104.9 3.5 %collective-permute-start.23 = (f32[4,132,2]{2,1,0:T(8,128)S(1)}, f32[4,132,2]{2,1,0:T(8,128)S(1)}, u32[]{:S(2)}, u32[]{:S(2)}) collective-permute-start(f32[4,132,2]{2,1,0:T(8,128)S(1)} %get-tuple-element.53), channel_id=1, source_target_pairs={{0,1},{1,2},{2,3},{3,4},{4,5},{5,6},{6,7},{7,0},{8,9},{9,10},{10,1... | collective-permute-start | bytes 12680 | tf_op jit(solution)/shard_map/ppermute | solution.py:18
  109.2 3.0 %copy-start.3 = (f32[4,128,128]{2,1,0:T(8,128)}, f32[4,128,128]{2,1,0:T(8,128)S(1)}, u32[]{:S(2)}) copy-start(f32[4,128,128]{2,1,0:T(8,128)S(1)} %fusion.75) | copy-start | bytes 786436
Sparse Core Ops, SparseCore 0:
  110.7 112.5 all-gather.2
